TPU v7x, 128 devices: a whole 4x4x4 slice. The times are simulated.
128 devices in a mesh: expert: 16 (over z, x), group: 8 (over y, core).
Axes of the slice: x: 4, y: 4, z: 4, core: 2. Of those that a mesh axis runs over, the one named last changes fastest.
Arguments:
- activations: bfloat16 [16384, 2048], P(('expert', 'group')), may hold values from -24 to 24
- out_grad: bfloat16 [16384, 2048], P(('expert', 'group')), may hold values from -24 to 24
- combine_weights: bfloat16 [16384, 4], P(('expert', 'group')), may hold values from 0.099609375 to 0.5
- expert_ids: int32 [16384, 4], P(('expert', 'group')), may hold values from 0 to 15, all different within a row; in each aligned block of 128 rows (0 to 127, 128 to 255, ...) at most 96 rows name the same one
- gate_up_weight: bfloat16 [16, 2048, 1024], P('expert'), may hold values from -0.125 to 0.125
- down_weight: bfloat16 [16, 2048, 512], P('expert'), may hold values from -0.25 to 0.25
Outputs:
- grad_input: bfloat16 [16384, 2048], P(('expert', 'group'))
- grad_combine: bfloat16 [16384, 4], P(('expert', 'group'))
- grad_gate_up: float32 [16, 2048, 1024], P('expert', 'group')
- grad_down: float32 [16, 2048, 512], P('expert', 'group')
Inputs may be any that keep to these rules, and one draw needn't show every extreme that they name: `expert_ids`: each row names 4 different experts. Within the 128 rows of one device no expert is named more than 96 times, and in some device's rows an expert is named exactly 96 times.
All inputs are finite; a program needn't handle non-finite values.
Results may differ from a plain program's by a relative error of at most 0.0064.
Values may be sent and summed in bfloat16 or wider, within the bound.
A program may use at most 128 MiB of HBM per device.

v0:
```python
import jax
import jax.numpy as jnp
from jax import lax
from jax.sharding import PartitionSpec as P


def body(activations, out_grad, combine_weights, expert_ids, gate_up_weight, down_weight):
    experts_all = lax.axis_size("expert")
    me = lax.axis_index("expert")
    columns = jnp.arange(experts_all, dtype=jnp.int32)
    named = expert_ids[:, :, None] == columns[None, None, :]
    table = jnp.sum(
        jnp.where(named, combine_weights.astype(jnp.float32)[:, :, None], 0.0), axis=1
    ).astype(jnp.bfloat16)
    rows_x = lax.all_gather(activations, "expert", axis=0, tiled=True)
    rows_g = lax.all_gather(out_grad, "expert", axis=0, tiled=True)
    tables = lax.all_gather(table, "expert", axis=0, tiled=True)
    mine = (columns == me).astype(jnp.float32)
    rows_w = jnp.sum(tables.astype(jnp.float32) * mine[None, :], axis=1, keepdims=True)
    weight_gu = gate_up_weight[0]
    weight_down = down_weight[0]
    hidden_dim = weight_down.shape[1]
    pre = jnp.dot(rows_x, weight_gu, preferred_element_type=jnp.float32)
    gate = pre[:, :hidden_dim]
    upper = pre[:, hidden_dim:]
    sig = jax.nn.sigmoid(gate)
    hidden = (gate * sig * upper).astype(jnp.bfloat16).astype(jnp.float32)
    raw = jnp.dot(rows_g, weight_down, preferred_element_type=jnp.float32)
    prob = jnp.sum(hidden * raw, axis=1, keepdims=True)
    hidden_grad = raw * rows_w
    gate_grad = hidden_grad * upper * sig * (1.0 + gate * (1.0 - sig))
    upper_grad = hidden_grad * gate * sig
    pre_grad = jnp.concatenate([gate_grad, upper_grad], axis=1).astype(jnp.bfloat16)
    scaled = (hidden * rows_w).astype(jnp.bfloat16)
    slot_grad = lax.dot_general(
        pre_grad, weight_gu, (((1,), (1,)), ((), ())), preferred_element_type=jnp.float32
    ).astype(jnp.bfloat16)
    grad_input = lax.psum_scatter(slot_grad, "expert", scatter_dimension=0, tiled=True)
    probs = lax.psum_scatter(
        (prob * mine[None, :]).astype(jnp.bfloat16), "expert", scatter_dimension=0, tiled=True
    )
    grad_combine = jnp.sum(
        jnp.where(named, probs.astype(jnp.float32)[:, None, :], 0.0), axis=2
    ).astype(jnp.bfloat16)
    grad_gate_up = lax.psum_scatter(
        lax.dot_general(
            rows_x, pre_grad, (((0,), (0,)), ((), ())), preferred_element_type=jnp.float32
        ).astype(jnp.bfloat16),
        "group",
        scatter_dimension=0,
        tiled=True,
    ).astype(jnp.float32)
    grad_down = lax.psum_scatter(
        lax.dot_general(
            rows_g, scaled, (((0,), (0,)), ((), ())), preferred_element_type=jnp.float32
        ).astype(jnp.bfloat16),
        "group",
        scatter_dimension=0,
        tiled=True,
    ).astype(jnp.float32)
    return (grad_input, grad_combine, grad_gate_up[None], grad_down[None])


def solution(mesh):
    rows = P(("expert", "group"), None)
    return jax.shard_map(
        body,
        mesh=mesh,
        in_specs=(rows, rows, rows, rows, P("expert", None, None), P("expert", None, None)),
        out_specs=(rows, rows, P("expert", "group", None), P("expert", "group", None)),
        check_vma=False,
    )
```

profile of v0, /device:TPU:0, one launch (start us, length us, event | category | flops | bytes accessed | tf_op | source)
XLA Modules:
  0.0 444.1 jit_solution(17004456806041273709)
XLA Ops:
  7.2 0.7 all-gather.5.cloned.1.call-update
  8.0 0.7 all-gather.3.cloned.1.call-update
  8.7 74.9 %all-gather.5.cloned.1.call-done = bf16[2048,2048]{1,0:T(8,128)(2,1)} async-done(((bf16[128,2048]{1,0:T(8,128)(2,1)}), bf16[2048,2048]{1,0:T(8,128)(2,1)}) %all-gather.5.cloned.1.call-update) | async-done | bytes 8388624 | tf_op jit(solution)/shard_map/all_gather | solution.py:15
  83.6 14.7 %fusion.3 = f32[2048,1024]{0,1:T(8,128)} fusion(bf16[2048,2048]{1,0:T(8,128)(2,1)} %all-gather.5.cloned.1.call-done, bf16[1,2048,1024]{2,1,0:T(8,128)(2,1)} %param.10), kind=kOutput, calls=%fused_computation.7 | convolution fusion | flops 8589934592 | bytes 20971520 | tf_op jit(solution)/shard_map/dot_general | solution.py:23
  98.2 58.0 %all-gather.3.cloned.1.call-done = bf16[2048,2048]{1,0:T(8,128)(2,1)} async-done(((bf16[128,2048]{1,0:T(8,128)(2,1)}), bf16[2048,2048]{1,0:T(8,128)(2,1)}) %all-gather.3.cloned.1.call-update) | async-done | bytes 8388624 | tf_op jit(solution)/shard_map/all_gather | solution.py:16
  156.3 11.9 %fusion = (f32[2048]{0:T(1024)S(1)}, bf16[2048,512]{0,1:T(8,128)(2,1)}, f32[2048,512]{0,1:T(8,128)}) fusion(f32[2048,1024]{0,1:T(8,128)} %fusion.3, bf16[2048,2048]{1,0:T(8,128)(2,1)} %all-gather.3.cloned.1.call-done, bf16[1,2048,512]{2,1,0:T(8,128)(2,1)S(1)} %copy-done), kind=kOutput, calls=%fused_computation.3 | convolution fusion | flops 4304402432 | bytes 25174016 | tf_op jit(solution)/shard_map/dot_general | solution.py:28
  168.2 1.0 copy.18
  169.3 73.2 %reduce-scatter.13.cloned.1.call-done = bf16[128,16]{1,0:T(8,128)(2,1)} async-done(((bf16[2048,16]{1,0:T(8,128)(2,1)}), bf16[128,16]{1,0:T(8,128)(2,1)}) %reduce-scatter.13.cloned.1.call-update) | async-done | bytes 4112
  242.6 0.8 copy.19
  243.4 0.6 select_reduce_fusion
  244.0 22.8 %all_gather.10 = bf16[2048,16]{0,1:T(8,128)(2,1)S(1)} all-gather(bf16[128,16]{0,1:T(8,128)(2,1)S(1)} %get-tuple-element.17), channel_id=1, replica_groups=mesh['expert'=16,'group'=8] {'expert'}, dimensions={0}, use_global_device_ids=true | all-gather | bytes 69632 | tf_op jit(solution)/shard_map/all_gather | solution.py:17
  266.9 9.9 %fusion.5 = bf16[2048,512]{0,1:T(8,128)(2,1)} fusion(bf16[2048,2048]{1,0:T(8,128)(2,1)} %all-gather.3.cloned.1.call-done, bf16[2048,512]{0,1:T(8,128)(2,1)} %get-tuple-element.19, f32[2048]{0:T(1024)S(1)} %multiply_reduce_fusion), kind=kOutput, calls=%fused_computation.15 | convolution fusion | flops 4299161600 | bytes 12591104 | tf_op jit(solution)/shard_map/dot_general | solution.py:54
  276.8 0.2 reduce-scatter.9.cloned.1.call-start
  277.0 5.7 %multiply_convert_fusion.2 = (bf16[2048,512]{0,1:T(8,128)(2,1)S(1)}, bf16[2048,512]{0,1:T(8,128)(2,1)S(1)}) fusion(f32[2048,1024]{0,1:T(8,128)} %fusion.3, f32[2048,512]{0,1:T(8,128)} %get-tuple-element.22, f32[2048]{0:T(1024)S(1)} %multiply_reduce_fusion), kind=kLoop, calls=%fused_computation.12 | loop fusion | flops 14680064 | bytes 16785408 | tf_op jit(solution)/shard_map/convert.2
  282.8 1.3 copy-done.1
  284.1 0.7 copy-done.2
  284.8 12.6 %convert_bitcast_fusion = bf16[2048,1024]{0,1:T(8,128)(2,1)} fusion(bf16[2048,2048]{1,0:T(8,128)(2,1)} %all-gather.5.cloned.1.call-done, bf16[2048,512]{0,1:T(8,128)(2,1)S(1)} %get-tuple-element.21, bf16[2048,512]{0,1:T(8,128)(2,1)S(1)} %get-tuple-element.20), kind=kOutput, calls=%fused_computation.9 | convolution fusion | flops 8600420352 | bytes 16777216 | tf_op jit(solution)/shard_map/dot_general | solution.py:46
  297.5 14.0 %convolution_convert_fusion = bf16[2048,2048]{1,0:T(8,128)(2,1)} fusion(bf16[1,2048,1024]{2,1,0:T(8,128)(2,1)} %param.10, bf16[2048,512]{0,1:T(8,128)(2,1)} %copy-done.2, bf16[2048,512]{0,1:T(8,128)(2,1)} %copy-done.1), kind=kOutput, calls=%fused_computation | convolution fusion | flops 8602517504 | bytes 16777216 | tf_op jit(solution)/shard_map/dot_general | solution.py:35
  311.6 1.0 bitcast_convert_fusion.1
  312.6 1.0 copy.17
  313.6 35.0 %reduce-scatter.9.cloned.1.call-done = bf16[256,1024]{0,1:T(8,128)(2,1)} async-done(((bf16[2048,1024]{0,1:T(8,128)(2,1)}), bf16[256,1024]{0,1:T(8,128)(2,1)}) %reduce-scatter.9.cloned.1.call-update) | async-done | bytes 524304 | tf_op jit(solution)/shard_map/reduce_scatter | solution.py:45
  348.5 1.1 bitcast_convert_fusion
  349.7 1.3 copy.16
  351.0 86.3 %reduce-scatter.7.cloned.1.call-done = bf16[128,2048]{1,0:T(8,128)(2,1)} async-done(((bf16[2048,2048]{1,0:T(8,128)(2,1)}), bf16[128,2048]{1,0:T(8,128)(2,1)}) %reduce-scatter.7.cloned.1.call-update) | async-done | bytes 524304 | tf_op jit(solution)/shard_map/reduce_scatter | solution.py:38
  (23 shorter events, 0.5 us)
Async XLA Ops:
  7.2 149.1 %copy-start = (bf16[1,2048,512]{2,1,0:T(8,128)(2,1)S(1)}, bf16[1,2048,512]{2,1,0:T(8,128)(2,1)}, u32[]{:S(2)}) copy-start(bf16[1,2048,512]{2,1,0:T(8,128)(2,1)} %param.11) | copy-start | bytes 6291460
  7.2 76.4 %all-gather.5.cloned.1.call-start = ((), (), s32[]{:S(2)}) async-start(), calls=%async_computation.5 | async-start | bytes 8912896 | tf_op jit(solution)/shard_map/all_gather | solution.py:15
  7.9 148.4 %all-gather.3.cloned.1.call-start = ((), (), s32[]{:S(2)}) async-start(), calls=%async_computation.4 | async-start | bytes 8912896 | tf_op jit(solution)/shard_map/all_gather | solution.py:16
  8.7 233.9 %reduce-scatter.13.cloned.1.call-start = ((), (), s32[]{:S(2)}) async-start(), calls=%async_computation.9 | async-start | bytes 557056
  98.2 71.1 %copy-start.4 = (bf16[128,4]{0,1:T(4,128)(2,1)S(1)}, bf16[128,4]{0,1:T(4,128)(2,1)}, u32[]{:S(2)}) copy-start(bf16[128,4]{0,1:T(4,128)(2,1)} %param.8) | copy-start | bytes 3076
  98.2 145.2 %copy-start.3 = (s32[128,4]{0,1:T(4,128)S(1)}, s32[128,4]{0,1:T(4,128)}, u32[]{:S(2)}) copy-start(s32[128,4]{0,1:T(4,128)} %param.9) | copy-start | bytes 6148
  169.3 142.3 %reduce-scatter.11.cloned.1.call-start = ((), (), s32[]{:S(2)}) async-start(), calls=%async_computation.8 | async-start | bytes 2359296 | tf_op jit(solution)/shard_map/reduce_scatter | solution.py:53
  276.8 71.7 %reduce-scatter.9.cloned.1.call-start = ((), (), s32[]{:S(2)}) async-start(), calls=%async_computation.7 | async-start | bytes 4718592 | tf_op jit(solution)/shard_map/reduce_scatter | solution.py:45
  282.8 1.3 copy-start.1
  282.8 2.0 copy-start.2
  297.5 139.8 %reduce-scatter.7.cloned.1.call-start = ((), (), s32[]{:S(2)}) async-start(), calls=%async_computation.6 | async-start | bytes 8912896 | tf_op jit(solution)/shard_map/reduce_scatter | solution.py:38
Sparse Core Ops, SparseCore 0:
  10.1 73.4 all-gather.4
  85.7 70.5 all-gather.2
  169.4 73.1 reduce-scatter.12
  276.9 32.4 reduce-scatter.10
  311.7 36.8 reduce-scatter.8
  352.4 84.8 reduce-scatter.6
where the time goes:
time: 444 us
  waiting for transfers between devices  329 us (74%)
  matrix products  63 us (14%)
  blocking collectives  22.8 us (5%)
  between operations  14.2 us (3%)
  other arithmetic  8.64 us (2%)
  local copies, waits for them, and re-layouts  6.14 us (1%)
    reduce_scatter x1, waiting for transfers between devices, body(): lax.psum_scatter(slot_grad, 'expert', scatter_dimension=0, tiled=True)  86.3 us
    all_gather x1, waiting for transfers between devices, body(): rows_x = lax.all_gather(activations, 'expert', axis=0, tiled=True)  74.9 us
    unnamed x7, waiting for transfers between devices  74.7 us
    all_gather x1, waiting for transfers between devices, body(): rows_g = lax.all_gather(out_grad, 'expert', axis=0, tiled=True)  58 us
    reduce_scatter x1, waiting for transfers between devices, body(): lax.psum_scatter(lax.dot_general(rows_x, pre_grad, (((0,), (0,)), ((), ()...  35 us
    all_gather x1, blocking collectives, body(): tables = lax.all_gather(table, 'expert', axis=0, tiled=True)  22.8 us
    dot_general x1, matrix products, body(): pre = jnp.dot(rows_x, weight_gu, preferred_element_type=jnp.float32)  14.7 us
    dot_general x1, matrix products, body(): lax.dot_general(pre_grad, weight_gu, (((1,), (1,)), ((), ())), preferred_...  14 us
  transfers between devices with their start and end apart: 6, of which 5 were waited for; matrix products, arithmetic and copies ran while one was open for 12% of the time, Pallas kernels for 0%

commit v1 on v0

--- a/solution.py
+++ b/solution.py
@@ -13,7 +13,24 @@
         jnp.where(named, combine_weights.astype(jnp.float32)[:, :, None], 0.0), axis=1
     ).astype(jnp.bfloat16)
     rows_x = lax.all_gather(activations, "expert", axis=0, tiled=True)
-    rows_g = lax.all_gather(out_grad, "expert", axis=0, tiled=True)
+    ways, here, step = (lax.axis_size("expert"), lax.axis_index("expert"), out_grad.shape[0])
+    lengths = [n * ways if d == 0 else n for d, n in enumerate(out_grad.shape)]
+    rows_g = lax.dynamic_update_slice_in_dim(
+        jnp.zeros(lengths, out_grad.dtype), out_grad, here * step, axis=0
+    )
+    going_up = going_down = out_grad
+    for far in range(1, ways // 2 + 1):
+        going_up = lax.ppermute(going_up, "expert", [(d, (d + 1) % ways) for d in range(ways)])
+        rows_g = lax.dynamic_update_slice_in_dim(
+            rows_g, going_up, (here - far) % ways * step, axis=0
+        )
+        if 2 * far < ways:
+            going_down = lax.ppermute(
+                going_down, "expert", [(d, (d - 1) % ways) for d in range(ways)]
+            )
+            rows_g = lax.dynamic_update_slice_in_dim(
+                rows_g, going_down, (here + far) % ways * step, axis=0
+            )
     tables = lax.all_gather(table, "expert", axis=0, tiled=True)
     mine = (columns == me).astype(jnp.float32)
     rows_w = jnp.sum(tables.astype(jnp.float32) * mine[None, :], axis=1, keepdims=True)

time: 444 us -> 464 us (1.045)
  waiting for transfers between devices: 329 us -> 286 us
  starting transfers between devices: 0.42 us -> 40.8 us
  local copies, waits for them, and re-layouts: 6.14 us -> 27.8 us
    ppermute x0 -> x15, waiting for transfers between devices: none -> 92.3 us  [the longest x8 85.5 us: body(): lax.ppermute(going_up, 'expert', [(d, (d + 1) % ways) for d in range(ways)])]
    all_gather x1, waiting for transfers between devices: 74.9 us -> 0.01 us  [body(): rows_x = lax.all_gather(activations, 'expert', axis=0, tiled=True)]
    all_gather x1 -> x0, waiting for transfers between devices: 58 us -> none  [body(): rows_g = lax.all_gather(out_grad, 'expert', axis=0, tiled=True)]
    ppermute x0 -> x15, starting transfers between devices: none -> 40.3 us  [the longest x7 38.6 us: body(): lax.ppermute(going_down, 'expert', [(d, (d - 1) % ways) for d in range(wa...]
    dynamic_update_slice x0 -> x16, local copies, waits for them, and re-layouts: none -> 18.8 us  [the longest x7 9.09 us: body(): lax.dynamic_update_slice_in_dim(rows_g, going_down, (here + far) % ways *...]
    unnamed x7 -> x6, waiting for transfers between devices: 74.7 us -> 71.5 us
  transfers between devices with their start and end apart: 6 -> 20, of which waited for: 5 -> 16; matrix products, arithmetic and copies ran while one was open for 12% -> 13% of each run, Pallas kernels for 0% -> 0%
where the time goes in v1:
time: 464 us
  waiting for transfers between devices  286 us (62%)
  matrix products  63.3 us (14%)
  starting transfers between devices  40.8 us (9%)
  local copies, waits for them, and re-layouts  27.8 us (6%)
  blocking collectives  23 us (5%)
  between operations  13.9 us (3%)
  other arithmetic  9.42 us (2%)
    reduce_scatter x1, waiting for transfers between devices, body(): lax.psum_scatter(slot_grad, 'expert', scatter_dimension=0, tiled=True)  86.5 us
    ppermute x8, waiting for transfers between devices, body(): lax.ppermute(going_up, 'expert', [(d, (d + 1) % ways) for d in range(ways)])  85.5 us
    unnamed x6, waiting for transfers between devices  71.5 us
    ppermute x7, starting transfers between devices, body(): lax.ppermute(going_down, 'expert', [(d, (d - 1) % ways) for d in range(wa...  38.6 us
    reduce_scatter x1, waiting for transfers between devices, body(): lax.psum_scatter(lax.dot_general(rows_x, pre_grad, (((0,), (0,)), ((), ()...  35.3 us
    all_gather x1, blocking collectives, body(): tables = lax.all_gather(table, 'expert', axis=0, tiled=True)  23 us
    dot_general x1, matrix products, body(): pre = jnp.dot(rows_x, weight_gu, preferred_element_type=jnp.float32)  14.5 us
    dot_general x1, matrix products, body(): lax.dot_general(pre_grad, weight_gu, (((1,), (1,)), ((), ())), preferred_...  14.2 us
  transfers between devices with their start and end apart: 20, of which 16 were waited for; matrix products, arithmetic and copies ran while one was open for 13% of the time, Pallas kernels for 0%

profile of v1, /device:TPU:0, one launch (start us, length us, event | category | flops | bytes accessed | tf_op | source)
XLA Modules:
  0.0 463.8 jit_solution(9645489228323069640)
XLA Ops:
  14.5 12.1 %collective-permute-done = bf16[128,2048]{1,0:T(8,128)(2,1)S(1)} collective-permute-done((bf16[128,2048]{1,0:T(8,128)(2,1)}, bf16[128,2048]{1,0:T(8,128)(2,1)S(1)}, u32[]{:S(2)}, u32[]{:S(2)}) %collective-permute-start) | collective-permute-done | bytes 524320 | tf_op jit(solution)/shard_map/ppermute | solution.py:23
  29.2 5.8 %collective-permute-start.3 = (bf16[128,2048]{1,0:T(8,128)(2,1)}, bf16[128,2048]{1,0:T(8,128)(2,1)}, u32[]{:S(2)}, u32[]{:S(2)}) collective-permute-start(bf16[128,2048]{1,0:T(8,128)(2,1)} %collective-permute-done.1), channel_id=1, source_target_pairs={{0,120},{8,0},{16,8},{24,16},{32,24},{40,32},{48,40},{56,48},{64,5... | collective-permute-start | bytes 1572872 | tf_op jit(solution)/shard_map/ppermute | solution.py:28
  35.0 13.8 %collective-permute-done.2 = bf16[128,2048]{1,0:T(8,128)(2,1)} collective-permute-done((bf16[128,2048]{1,0:T(8,128)(2,1)S(1)}, bf16[128,2048]{1,0:T(8,128)(2,1)}, u32[]{:S(2)}, u32[]{:S(2)}) %collective-permute-start.2) | collective-permute-done | bytes 524320 | tf_op jit(solution)/shard_map/ppermute | solution.py:23
  48.8 5.3 %collective-permute-start.5 = (bf16[128,2048]{1,0:T(8,128)(2,1)}, bf16[128,2048]{1,0:T(8,128)(2,1)}, u32[]{:S(2)}, u32[]{:S(2)}) collective-permute-start(bf16[128,2048]{1,0:T(8,128)(2,1)} %collective-permute-done.3), channel_id=1, source_target_pairs={{0,120},{8,0},{16,8},{24,16},{32,24},{40,32},{48,40},{56,48},{64,5... | collective-permute-start | bytes 1572872 | tf_op jit(solution)/shard_map/ppermute | solution.py:28
  59.5 11.3 %collective-permute-done.4 = bf16[128,2048]{1,0:T(8,128)(2,1)S(1)} collective-permute-done((bf16[128,2048]{1,0:T(8,128)(2,1)}, bf16[128,2048]{1,0:T(8,128)(2,1)S(1)}, u32[]{:S(2)}, u32[]{:S(2)}) %collective-permute-start.4) | collective-permute-done | bytes 524320 | tf_op jit(solution)/shard_map/ppermute | solution.py:23
  75.4 5.8 %collective-permute-start.7 = (bf16[128,2048]{1,0:T(8,128)(2,1)}, bf16[128,2048]{1,0:T(8,128)(2,1)S(1)}, u32[]{:S(2)}, u32[]{:S(2)}) collective-permute-start(bf16[128,2048]{1,0:T(8,128)(2,1)} %collective-permute-done.5), channel_id=1, source_target_pairs={{0,120},{8,0},{16,8},{24,16},{32,24},{40,32},{48,40},{56,48},{64,5... | collective-permute-start | bytes 1572872 | tf_op jit(solution)/shard_map/ppermute | solution.py:28
  83.1 15.1 %collective-permute-done.6 = bf16[128,2048]{1,0:T(8,128)(2,1)S(1)} collective-permute-done((bf16[128,2048]{1,0:T(8,128)(2,1)S(1)}, bf16[128,2048]{1,0:T(8,128)(2,1)S(1)}, u32[]{:S(2)}, u32[]{:S(2)}) %collective-permute-start.6) | collective-permute-done | bytes 524320 | tf_op jit(solution)/shard_map/ppermute | solution.py:23
  103.1 5.7 %collective-permute-start.9 = (bf16[128,2048]{1,0:T(8,128)(2,1)S(1)}, bf16[128,2048]{1,0:T(8,128)(2,1)S(1)}, u32[]{:S(2)}, u32[]{:S(2)}) collective-permute-start(bf16[128,2048]{1,0:T(8,128)(2,1)S(1)} %collective-permute-done.7), channel_id=1, source_target_pairs={{0,120},{8,0},{16,8},{24,16},{32,24},{40,32},{48,40},{56,48},{64,5... | collective-permute-start | bytes 1572872 | tf_op jit(solution)/shard_map/ppermute | solution.py:28
  109.6 12.0 %collective-permute-done.8 = bf16[128,2048]{1,0:T(8,128)(2,1)S(1)} collective-permute-done((bf16[128,2048]{1,0:T(8,128)(2,1)S(1)}, bf16[128,2048]{1,0:T(8,128)(2,1)S(1)}, u32[]{:S(2)}, u32[]{:S(2)}) %collective-permute-start.8) | collective-permute-done | bytes 524320 | tf_op jit(solution)/shard_map/ppermute | solution.py:23
  124.4 5.4 %collective-permute-start.11 = (bf16[128,2048]{1,0:T(8,128)(2,1)S(1)}, bf16[128,2048]{1,0:T(8,128)(2,1)S(1)}, u32[]{:S(2)}, u32[]{:S(2)}) collective-permute-start(bf16[128,2048]{1,0:T(8,128)(2,1)S(1)} %collective-permute-done.9), channel_id=1, source_target_pairs={{0,120},{8,0},{16,8},{24,16},{32,24},{40,32},{48,40},{56,48},{64,5... | collective-permute-start | bytes 1572872 | tf_op jit(solution)/shard_map/ppermute | solution.py:28
  130.6 5.7 %collective-permute-done.10 = bf16[128,2048]{1,0:T(8,128)(2,1)S(1)} collective-permute-done((bf16[128,2048]{1,0:T(8,128)(2,1)S(1)}, bf16[128,2048]{1,0:T(8,128)(2,1)S(1)}, u32[]{:S(2)}, u32[]{:S(2)}) %collective-permute-start.10) | collective-permute-done | bytes 524320 | tf_op jit(solution)/shard_map/ppermute | solution.py:23
  138.3 5.8 %collective-permute-start.13 = (bf16[128,2048]{1,0:T(8,128)(2,1)S(1)}, bf16[128,2048]{1,0:T(8,128)(2,1)S(1)}, u32[]{:S(2)}, u32[]{:S(2)}) collective-permute-start(bf16[128,2048]{1,0:T(8,128)(2,1)S(1)} %collective-permute-done.11), channel_id=1, source_target_pairs={{0,120},{8,0},{16,8},{24,16},{32,24},{40,32},{48,40},{56,48},{64,5... | collective-permute-start | bytes 1572872 | tf_op jit(solution)/shard_map/ppermute | solution.py:28
  145.0 5.1 %collective-permute-done.12 = bf16[128,2048]{1,0:T(8,128)(2,1)S(1)} collective-permute-done((bf16[128,2048]{1,0:T(8,128)(2,1)S(1)}, bf16[128,2048]{1,0:T(8,128)(2,1)S(1)}, u32[]{:S(2)}, u32[]{:S(2)}) %collective-permute-start.12) | collective-permute-done | bytes 524320 | tf_op jit(solution)/shard_map/ppermute | solution.py:23
  152.7 10.4 %collective-permute-done.14 = bf16[128,2048]{1,0:T(8,128)(2,1)S(1)} collective-permute-done((bf16[128,2048]{1,0:T(8,128)(2,1)S(1)}, bf16[128,2048]{1,0:T(8,128)(2,1)S(1)}, u32[]{:S(2)}, u32[]{:S(2)}) %collective-permute-start.14) | collective-permute-done | bytes 524320 | tf_op jit(solution)/shard_map/ppermute | solution.py:23
  163.9 14.5 %fusion.3 = f32[2048,1024]{0,1:T(8,128)} fusion(bf16[2048,2048]{1,0:T(8,128)(2,1)} %all-gather.2.cloned.1.call-done, bf16[1,2048,1024]{2,1,0:T(8,128)(2,1)} %param.10), kind=kOutput, calls=%fused_computation.7 | convolution fusion | flops 8589934592 | bytes 20971520 | tf_op jit(solution)/shard_map/dot_general | solution.py:40
  178.5 11.9 %fusion = (f32[2048]{0:T(1024)S(1)}, bf16[2048,512]{0,1:T(8,128)(2,1)}, f32[2048,512]{0,1:T(8,128)}) fusion(f32[2048,1024]{0,1:T(8,128)} %fusion.3, bf16[2048,2048]{1,0:T(8,128)(2,1)} %constant_dynamic-update-slice_fusion, bf16[1,2048,512]{2,1,0:T(8,128)(2,1)S(1)} %copy-done), kind=kOutput, calls=%fused_computation.3 | convolution fusion | flops 4304402432 | bytes 25174016 | tf_op jit(solution)/shard_map/dot_general | solution.py:45
  191.5 70.8 %reduce-scatter.13.cloned.1.call-done = bf16[128,16]{1,0:T(8,128)(2,1)} async-done(((bf16[2048,16]{1,0:T(8,128)(2,1)}), bf16[128,16]{1,0:T(8,128)(2,1)}) %reduce-scatter.13.cloned.1.call-update) | async-done | bytes 4112
  263.7 23.0 %all_gather.6 = bf16[2048,16]{0,1:T(8,128)(2,1)S(1)} all-gather(bf16[128,16]{0,1:T(8,128)(2,1)S(1)} %get-tuple-element.17), channel_id=1, replica_groups=mesh['expert'=16,'group'=8] {'expert'}, dimensions={0}, use_global_device_ids=true | all-gather | bytes 69632 | tf_op jit(solution)/shard_map/all_gather | solution.py:34
  286.8 9.9 %convolution_convert_fusion.1 = bf16[2048,512]{1,0:T(8,128)(2,1)} fusion(bf16[2048,2048]{1,0:T(8,128)(2,1)} %constant_dynamic-update-slice_fusion, bf16[2048,512]{0,1:T(8,128)(2,1)} %get-tuple-element.19, f32[2048]{0:T(1024)S(1)} %multiply_reduce_fusion), kind=kOutput, calls=%fused_computation.14 | convolution fusion | flops 4299161600 | bytes 12591104 | tf_op jit(solution)/shard_map/dot_general | solution.py:71
  296.8 5.7 %multiply_convert_fusion.2 = (bf16[2048,512]{0,1:T(8,128)(2,1)S(1)}, bf16[2048,512]{0,1:T(8,128)(2,1)S(1)}) fusion(f32[2048,1024]{0,1:T(8,128)} %fusion.3, f32[2048,512]{0,1:T(8,128)} %get-tuple-element.22, f32[2048]{0:T(1024)S(1)} %multiply_reduce_fusion), kind=kLoop, calls=%fused_computation.12 | loop fusion | flops 14680064 | bytes 16785408 | tf_op jit(solution)/shard_map/convert.2
  303.9 12.8 %convert_bitcast_fusion = bf16[2048,1024]{0,1:T(8,128)(2,1)} fusion(bf16[2048,2048]{1,0:T(8,128)(2,1)} %all-gather.2.cloned.1.call-done, bf16[2048,512]{0,1:T(8,128)(2,1)S(1)} %get-tuple-element.21, bf16[2048,512]{0,1:T(8,128)(2,1)S(1)} %get-tuple-element.20), kind=kOutput, calls=%fused_computation.9 | convolution fusion | flops 8600420352 | bytes 16777216 | tf_op jit(solution)/shard_map/dot_general | solution.py:63
  317.1 14.2 %convolution_convert_fusion = bf16[2048,2048]{1,0:T(8,128)(2,1)} fusion(bf16[1,2048,1024]{2,1,0:T(8,128)(2,1)} %param.10, bf16[2048,512]{0,1:T(8,128)(2,1)} %copy-done.3, bf16[2048,512]{0,1:T(8,128)(2,1)} %copy-done.2), kind=kOutput, calls=%fused_computation | convolution fusion | flops 8602517504 | bytes 16777216 | tf_op jit(solution)/shard_map/dot_general | solution.py:52
  333.1 35.3 %reduce-scatter.9.cloned.1.call-done = bf16[256,1024]{0,1:T(8,128)(2,1)} async-done(((bf16[2048,1024]{0,1:T(8,128)(2,1)}), bf16[256,1024]{0,1:T(8,128)(2,1)}) %reduce-scatter.9.cloned.1.call-update) | async-done | bytes 524304 | tf_op jit(solution)/shard_map/reduce_scatter | solution.py:62
  370.8 86.5 %reduce-scatter.7.cloned.1.call-done = bf16[128,2048]{1,0:T(8,128)(2,1)} async-done(((bf16[2048,2048]{1,0:T(8,128)(2,1)}), bf16[128,2048]{1,0:T(8,128)(2,1)}) %reduce-scatter.7.cloned.1.call-update) | async-done | bytes 524304 | tf_op jit(solution)/shard_map/reduce_scatter | solution.py:55
  (72 shorter events, 46.0 us)
Async XLA Ops:
  7.2 171.3 %copy-start = (bf16[1,2048,512]{2,1,0:T(8,128)(2,1)S(1)}, bf16[1,2048,512]{2,1,0:T(8,128)(2,1)}, u32[]{:S(2)}) copy-start(bf16[1,2048,512]{2,1,0:T(8,128)(2,1)} %param.11) | copy-start | bytes 6291460
  7.2 51.5 %copy-start.4 = (bf16[128,2048]{1,0:T(8,128)(2,1)S(1)}, bf16[128,2048]{1,0:T(8,128)(2,1)}, u32[]{:S(2)}) copy-start(bf16[128,2048]{1,0:T(8,128)(2,1)} %param.7) | copy-start | bytes 1572868
  7.2 156.7 %all-gather.2.cloned.1.call-start = ((), (), s32[]{:S(2)}) async-start(), calls=%async_computation.4 | async-start | bytes 8912896 | tf_op jit(solution)/shard_map/all_gather | solution.py:15
  7.9 254.4 %reduce-scatter.13.cloned.1.call-start = ((), (), s32[]{:S(2)}) async-start(), calls=%async_computation.8 | async-start | bytes 557056
  8.0 18.5 %collective-permute-start = (bf16[128,2048]{1,0:T(8,128)(2,1)}, bf16[128,2048]{1,0:T(8,128)(2,1)S(1)}, u32[]{:S(2)}, u32[]{:S(2)}) collective-permute-start(bf16[128,2048]{1,0:T(8,128)(2,1)} %param.7), channel_id=1, source_target_pairs={{0,8},{8,16},{16,24},{24,32},{32,40},{40,48},{48,56},{56,64},{64,7... | collective-permute-start | bytes 1572872 | tf_op jit(solution)/shard_map/ppermute | solution.py:23
  9.6 19.5 %collective-permute-start.1 = (bf16[128,2048]{1,0:T(8,128)(2,1)}, bf16[128,2048]{1,0:T(8,128)(2,1)}, u32[]{:S(2)}, u32[]{:S(2)}) collective-permute-start(bf16[128,2048]{1,0:T(8,128)(2,1)} %param.7), channel_id=1, source_target_pairs={{0,120},{8,0},{16,8},{24,16},{32,24},{40,32},{48,40},{56,48},{64,5... | collective-permute-start | bytes 1572872 | tf_op jit(solution)/shard_map/ppermute | solution.py:28
  26.5 22.3 %collective-permute-start.2 = (bf16[128,2048]{1,0:T(8,128)(2,1)S(1)}, bf16[128,2048]{1,0:T(8,128)(2,1)}, u32[]{:S(2)}, u32[]{:S(2)}) collective-permute-start(bf16[128,2048]{1,0:T(8,128)(2,1)S(1)} %collective-permute-done), channel_id=1, source_target_pairs={{0,8},{8,16},{16,24},{24,32},{32,40},{40,48},{48,56},{56,64},{64,7... | collective-permute-start | bytes 1572872 | tf_op jit(solution)/shard_map/ppermute | solution.py:23
  29.2 19.6 %collective-permute-start.3 = (bf16[128,2048]{1,0:T(8,128)(2,1)}, bf16[128,2048]{1,0:T(8,128)(2,1)}, u32[]{:S(2)}, u32[]{:S(2)}) collective-permute-start(bf16[128,2048]{1,0:T(8,128)(2,1)} %collective-permute-done.1), channel_id=1, source_target_pairs={{0,120},{8,0},{16,8},{24,16},{32,24},{40,32},{48,40},{56,48},{64,5... | collective-permute-start | bytes 1572872 | tf_op jit(solution)/shard_map/ppermute | solution.py:28
  48.8 22.0 %collective-permute-start.4 = (bf16[128,2048]{1,0:T(8,128)(2,1)}, bf16[128,2048]{1,0:T(8,128)(2,1)S(1)}, u32[]{:S(2)}, u32[]{:S(2)}) collective-permute-start(bf16[128,2048]{1,0:T(8,128)(2,1)} %collective-permute-done.2), channel_id=1, source_target_pairs={{0,8},{8,16},{16,24},{24,32},{32,40},{40,48},{48,56},{56,64},{64,7... | collective-permute-start | bytes 1572872 | tf_op jit(solution)/shard_map/ppermute | solution.py:23
  48.8 26.6 %collective-permute-start.5 = (bf16[128,2048]{1,0:T(8,128)(2,1)}, bf16[128,2048]{1,0:T(8,128)(2,1)}, u32[]{:S(2)}, u32[]{:S(2)}) collective-permute-start(bf16[128,2048]{1,0:T(8,128)(2,1)} %collective-permute-done.3), channel_id=1, source_target_pairs={{0,120},{8,0},{16,8},{24,16},{32,24},{40,32},{48,40},{56,48},{64,5... | collective-permute-start | bytes 1572872 | tf_op jit(solution)/shard_map/ppermute | solution.py:28
  70.8 27.4 %collective-permute-start.6 = (bf16[128,2048]{1,0:T(8,128)(2,1)S(1)}, bf16[128,2048]{1,0:T(8,128)(2,1)S(1)}, u32[]{:S(2)}, u32[]{:S(2)}) collective-permute-start(bf16[128,2048]{1,0:T(8,128)(2,1)S(1)} %collective-permute-done.4), channel_id=1, source_target_pairs={{0,8},{8,16},{16,24},{24,32},{32,40},{40,48},{48,56},{56,64},{64,7... | collective-permute-start | bytes 1572872 | tf_op jit(solution)/shard_map/ppermute | solution.py:23
  75.4 27.7 %collective-permute-start.7 = (bf16[128,2048]{1,0:T(8,128)(2,1)}, bf16[128,2048]{1,0:T(8,128)(2,1)S(1)}, u32[]{:S(2)}, u32[]{:S(2)}) collective-permute-start(bf16[128,2048]{1,0:T(8,128)(2,1)} %collective-permute-done.5), channel_id=1, source_target_pairs={{0,120},{8,0},{16,8},{24,16},{32,24},{40,32},{48,40},{56,48},{64,5... | collective-permute-start | bytes 1572872 | tf_op jit(solution)/shard_map/ppermute | solution.py:28
  98.3 23.4 %collective-permute-start.8 = (bf16[128,2048]{1,0:T(8,128)(2,1)S(1)}, bf16[128,2048]{1,0:T(8,128)(2,1)S(1)}, u32[]{:S(2)}, u32[]{:S(2)}) collective-permute-start(bf16[128,2048]{1,0:T(8,128)(2,1)S(1)} %collective-permute-done.6), channel_id=1, source_target_pairs={{0,8},{8,16},{16,24},{24,32},{32,40},{40,48},{48,56},{56,64},{64,7... | collective-permute-start | bytes 1572872 | tf_op jit(solution)/shard_map/ppermute | solution.py:23
  103.1 21.3 %collective-permute-start.9 = (bf16[128,2048]{1,0:T(8,128)(2,1)S(1)}, bf16[128,2048]{1,0:T(8,128)(2,1)S(1)}, u32[]{:S(2)}, u32[]{:S(2)}) collective-permute-start(bf16[128,2048]{1,0:T(8,128)(2,1)S(1)} %collective-permute-done.7), channel_id=1, source_target_pairs={{0,120},{8,0},{16,8},{24,16},{32,24},{40,32},{48,40},{56,48},{64,5... | collective-permute-start | bytes 1572872 | tf_op jit(solution)/shard_map/ppermute | solution.py:28
  121.6 14.7 %collective-permute-start.10 = (bf16[128,2048]{1,0:T(8,128)(2,1)S(1)}, bf16[128,2048]{1,0:T(8,128)(2,1)S(1)}, u32[]{:S(2)}, u32[]{:S(2)}) collective-permute-start(bf16[128,2048]{1,0:T(8,128)(2,1)S(1)} %collective-permute-done.8), channel_id=1, source_target_pairs={{0,8},{8,16},{16,24},{24,32},{32,40},{40,48},{48,56},{56,64},{64,7... | collective-permute-start | bytes 1572872 | tf_op jit(solution)/shard_map/ppermute | solution.py:23
  124.4 14.0 %collective-permute-start.11 = (bf16[128,2048]{1,0:T(8,128)(2,1)S(1)}, bf16[128,2048]{1,0:T(8,128)(2,1)S(1)}, u32[]{:S(2)}, u32[]{:S(2)}) collective-permute-start(bf16[128,2048]{1,0:T(8,128)(2,1)S(1)} %collective-permute-done.9), channel_id=1, source_target_pairs={{0,120},{8,0},{16,8},{24,16},{32,24},{40,32},{48,40},{56,48},{64,5... | collective-permute-start | bytes 1572872 | tf_op jit(solution)/shard_map/ppermute | solution.py:28
  136.3 13.8 %collective-permute-start.12 = (bf16[128,2048]{1,0:T(8,128)(2,1)S(1)}, bf16[128,2048]{1,0:T(8,128)(2,1)S(1)}, u32[]{:S(2)}, u32[]{:S(2)}) collective-permute-start(bf16[128,2048]{1,0:T(8,128)(2,1)S(1)} %collective-permute-done.10), channel_id=1, source_target_pairs={{0,8},{8,16},{16,24},{24,32},{32,40},{40,48},{48,56},{56,64},{64,7... | collective-permute-start | bytes 1572872 | tf_op jit(solution)/shard_map/ppermute | solution.py:23
  138.3 13.5 %collective-permute-start.13 = (bf16[128,2048]{1,0:T(8,128)(2,1)S(1)}, bf16[128,2048]{1,0:T(8,128)(2,1)S(1)}, u32[]{:S(2)}, u32[]{:S(2)}) collective-permute-start(bf16[128,2048]{1,0:T(8,128)(2,1)S(1)} %collective-permute-done.11), channel_id=1, source_target_pairs={{0,120},{8,0},{16,8},{24,16},{32,24},{40,32},{48,40},{56,48},{64,5... | collective-permute-start | bytes 1572872 | tf_op jit(solution)/shard_map/ppermute | solution.py:28
  150.1 13.0 %collective-permute-start.14 = (bf16[128,2048]{1,0:T(8,128)(2,1)S(1)}, bf16[128,2048]{1,0:T(8,128)(2,1)S(1)}, u32[]{:S(2)}, u32[]{:S(2)}) collective-permute-start(bf16[128,2048]{1,0:T(8,128)(2,1)S(1)} %collective-permute-done.12), channel_id=1, source_target_pairs={{0,8},{8,16},{16,24},{24,32},{32,40},{40,48},{48,56},{56,64},{64,7... | collective-permute-start | bytes 1572872 | tf_op jit(solution)/shard_map/ppermute | solution.py:23
  178.5 84.6 %copy-start.6 = (s32[128,4]{0,1:T(4,128)S(1)}, s32[128,4]{0,1:T(4,128)}, u32[]{:S(2)}) copy-start(s32[128,4]{0,1:T(4,128)} %param.9) | copy-start | bytes 6148
  191.5 139.8 %reduce-scatter.11.cloned.1.call-start = ((), (), s32[]{:S(2)}) async-start(), calls=%async_computation.7 | async-start | bytes 2359296 | tf_op jit(solution)/shard_map/reduce_scatter | solution.py:70
  296.8 71.6 %reduce-scatter.9.cloned.1.call-start = ((), (), s32[]{:S(2)}) async-start(), calls=%async_computation.6 | async-start | bytes 4718592 | tf_op jit(solution)/shard_map/reduce_scatter | solution.py:62
  316.7 140.6 %reduce-scatter.7.cloned.1.call-start = ((), (), s32[]{:S(2)}) async-start(), calls=%async_computation.5 | async-start | bytes 8912896 | tf_op jit(solution)/shard_map/reduce_scatter | solution.py:55
  317.1 140.2 %copy-start.1 = (bf16[1,2048,512]{2,1,0:T(8,128)(2,1)S(1)}, bf16[1,2048,512]{2,1,0:T(8,128)(2,1)}, u32[]{:S(2)}) copy-start(bf16[1,2048,512]{2,1,0:T(8,128)(2,1)} %param.11) | copy-start | bytes 6291460
  (4 other events, 37.0 us)
Sparse Core Ops, SparseCore 0:
  10.1 110.0 all-gather.1
  191.6 70.6 reduce-scatter.12
  296.9 32.5 reduce-scatter.10
  331.7 36.6 reduce-scatter.8
  372.2 85.0 reduce-scatter.6
